TPU v7x, 32 devices: a whole 2x2x4 slice. The times are simulated.
32 devices in a mesh: req: 16 (over z, y, core), grp: 2 (over x).
Axes of the slice: x: 2, y: 2, z: 4, core: 2. Of those that a mesh axis runs over, the one named last changes fastest.
Arguments:
- tokens: bfloat16 [8192, 1024], P('req'), may hold values from -6 to 6
- norm_attn: float32 [1024], replicated, may hold values from 0.25 to 1.75
- w_query: bfloat16 [1024, 1024], P(None, 'grp'), may hold values from -0.1875 to 0.1875
- w_key: bfloat16 [1024, 1024], P(None, 'grp'), may hold values from -0.1875 to 0.1875
- w_value: bfloat16 [1024, 1024], P(None, 'grp'), may hold values from -0.1875 to 0.1875
- w_out: bfloat16 [1024, 1024], P('grp'), may hold values from -0.1875 to 0.1875
- persist_keys: bfloat16 [16, 1024], P(None, 'grp'), may hold values from -5 to 5
- persist_values: bfloat16 [16, 1024], P(None, 'grp'), may hold values from -5 to 5
- kv_cache: bfloat16 [768, 2, 128, 1024], P('req', None, None, 'grp'), may hold values from -160 to 160
- slot_request: int32 [768], P('req'), may hold values from 0 to 255, as said below
- slot_page: int32 [768], P('req'), may hold values from 0 to 48, as said below
- cache_len: int32 [256], P('req'), may hold values from 1 to 2304
- tree_mask: int32 [256, 32, 32], P('req'), may hold values from 0 to 1, as said below
- accept_path: int32 [256, 8], P('req'), may hold values from 0 to 31, as said below
- accept_len: int32 [256], P('req'), may hold values from 1 to 8
- memory: float32 [256, 8, 128, 128], P('req', 'grp'), may hold values from -4 to 4
- momentum: float32 [256, 8, 128, 128], P('req', 'grp'), may hold values from -1.2 to 1.2
- momentum_code: int32 [256, 8, 8], P('req', None, 'grp'), may hold values from 0 to 15
- forget_code: int32 [256, 8, 8], P('req', None, 'grp'), may hold values from 0 to 15
- norm_ffn: float32 [1024], replicated, may hold values from 0.25 to 1.75
- w_gate_up: bfloat16 [2, 1024, 2816], P(None, None, 'grp'), may hold values from -0.1875 to 0.1875
- w_down: bfloat16 [2816, 1024], P('grp'), may hold values from -0.109375 to 0.109375
Outputs:
- layer_out: bfloat16 [8192, 1024], P(('req', 'grp'))
- memory_out: float32 [256, 8, 128, 128], P('req', 'grp')
- momentum_out: float32 [256, 8, 128, 128], P('req', 'grp')
Inputs may be any that keep to these rules, and one draw needn't show every extreme that they name: `slot_request`: slot s lies with index s // 48 of req; slots s with (s % 48) // 3 = j hold pages of requests j * 16 to (j + 1) * 16 - 1 only. The live pages 0 .. ceil(cache_len[r] / 128) - 1 of every request stand each in exactly one slot; every other slot has page number 16 * 3. `slot_page`: see slot_request. `tree_mask`: each node's parent precedes it; node 0 is the root; rows include the node itself. `accept_path`: entry n is the node at depth n on the root path of one draft node.
All inputs are finite; a program needn't handle non-finite values.
Results may differ from a plain program's by a relative error of at most 0.015.
Values may be sent and summed in bfloat16 or wider, within the bound.
No kernel may reach another device: no remote copies, remote signals or barrier semaphores. Data moves between devices by JAX's collectives and lax.ppermute only.
A program may use at most 192 MiB of HBM per device.

v0:
```python
import math
import jax
import jax.numpy as jnp
from jax import lax
from jax.sharding import PartitionSpec as P

HD = 128
EPS = 1e-06
THETA = 0.5
NEG = -1e30


def rms_norm(rows, gain):
    values = rows.astype(jnp.float32)
    factor = lax.rsqrt(jnp.mean(values * values, axis=-1, keepdims=True) + EPS)
    return (values * factor * gain).astype(jnp.bfloat16)


def unit_rows(vectors):
    return vectors * lax.rsqrt(jnp.sum(vectors * vectors, axis=-1, keepdims=True) + EPS)


def page_partials(pages, page_queries, page_first, page_limit, scale):
    count = pages.shape[0]
    page_len = pages.shape[2]
    width = pages.shape[3]
    heads = width // HD
    draft = page_queries.shape[1]
    query_four = page_queries.reshape(count, draft, heads, HD)
    key_four = pages[:, 0].reshape(count, page_len, heads, HD)
    value_four = pages[:, 1].reshape(count, page_len, heads, HD)
    scores = (
        jnp.einsum("sihd,sthd->shit", query_four, key_four, preferred_element_type=jnp.float32)
        * scale
    )
    position = page_first[:, None] + jnp.arange(page_len, dtype=jnp.int32)[None, :]
    valid = (position < page_limit[:, None])[:, None, None, :]
    masked = jnp.where(valid, scores, NEG)
    top = jnp.max(masked, axis=3)
    weight = jnp.where(valid, jnp.exp(masked - top[..., None]), 0.0)
    total = jnp.sum(weight, axis=3)
    numer = jnp.einsum(
        "shit,sthd->sihd",
        weight.astype(jnp.bfloat16),
        value_four,
        preferred_element_type=jnp.float32,
    )
    return (numer.reshape(count, draft, width), top, total)


def on_device(
    tokens,
    norm_attn,
    w_query,
    w_key,
    w_value,
    w_out,
    persist_keys,
    persist_values,
    kv_cache,
    slot_request,
    slot_page,
    cache_len,
    tree_mask,
    accept_path,
    accept_len,
    memory,
    momentum,
    momentum_code,
    forget_code,
    norm_ffn,
    w_gate_up,
    w_down,
):
    group_rows = tokens.shape[0]
    reqs = cache_len.shape[0]
    draft = tree_mask.shape[1]
    width = w_query.shape[1]
    heads = width // HD
    fixed_count = persist_keys.shape[0]
    page_len = kv_cache.shape[2]
    scale = 1.0 / math.sqrt(HD)
    normed = rms_norm(tokens, norm_attn)
    queries = jnp.dot(normed, w_query, preferred_element_type=jnp.float32).astype(jnp.bfloat16)
    keys = jnp.dot(normed, w_key, preferred_element_type=jnp.float32).astype(jnp.bfloat16)
    values = jnp.dot(normed, w_value, preferred_element_type=jnp.float32).astype(jnp.bfloat16)
    query_four = queries.reshape(reqs, draft, heads, HD)
    key_four = keys.reshape(reqs, draft, heads, HD)
    value_four = values.reshape(reqs, draft, heads, HD)
    fixed_keys = persist_keys.reshape(fixed_count, heads, HD)
    fixed_values = persist_values.reshape(fixed_count, heads, HD)
    tree_scores = (
        jnp.einsum("rihd,rjhd->rhij", query_four, key_four, preferred_element_type=jnp.float32)
        * scale
    )
    tree_scores = jnp.where(tree_mask[:, None] == 1, tree_scores, NEG)
    fixed_scores = (
        jnp.einsum("rihd,phd->rhip", query_four, fixed_keys, preferred_element_type=jnp.float32)
        * scale
    )
    local_scores = jnp.concatenate([fixed_scores, tree_scores], axis=3)
    local_top = jnp.max(local_scores, axis=3)
    local_weight = jnp.exp(local_scores - local_top[..., None])
    local_total = jnp.sum(local_weight, axis=3)
    local_rounded = local_weight.astype(jnp.bfloat16)
    local_numer = jnp.einsum(
        "rhip,phd->rihd",
        local_rounded[..., :fixed_count],
        fixed_values,
        preferred_element_type=jnp.float32,
    )
    local_numer = local_numer + jnp.einsum(
        "rhij,rjhd->rihd",
        local_rounded[..., fixed_count:],
        value_four,
        preferred_element_type=jnp.float32,
    )
    first_request = lax.axis_index("req") * reqs
    request_ids = jnp.arange(reqs, dtype=jnp.int32)
    moved_pages, moved_request, moved_page = (
        lax.all_to_all(kv_cache, "req", split_axis=0, concat_axis=0, tiled=True),
        lax.all_to_all(slot_request, "req", split_axis=0, concat_axis=0, tiled=True),
        lax.all_to_all(slot_page, "req", split_axis=0, concat_axis=0, tiled=True),
    )
    local_request = moved_request - first_request
    pick = local_request[:, None] == request_ids[None, :]
    limits = jnp.sum(jnp.where(pick, cache_len[None, :], 0), axis=1)
    page_queries = queries.reshape(reqs, draft, width)[local_request]
    numer, top, total = page_partials(
        moved_pages, page_queries, moved_page * page_len, limits, scale
    )
    slot_count = numer.shape[0]
    pick_weight = pick.astype(jnp.float32)
    request_top = jnp.max(jnp.where(pick[:, :, None, None], top[:, None], NEG), axis=0)
    best = jnp.maximum(request_top, local_top)
    slot_best = jnp.einsum("sr,rhi->shi", pick_weight, best, precision=lax.Precision.HIGHEST)
    factor = jnp.exp(top - slot_best)
    scaled = (
        numer.reshape(slot_count, draft, heads, HD) * jnp.transpose(factor, (0, 2, 1))[..., None]
    )
    page_numer = jnp.einsum("sr,sihd->rihd", pick_weight, scaled, precision=lax.Precision.HIGHEST)
    page_total = jnp.einsum(
        "sr,shi->rhi", pick_weight, total * factor, precision=lax.Precision.HIGHEST
    )
    local_factor = jnp.exp(local_top - best)
    numer_all = local_numer * jnp.transpose(local_factor, (0, 2, 1))[..., None] + page_numer
    total_all = local_total * local_factor + page_total
    attention = numer_all / jnp.transpose(total_all, (0, 2, 1))[..., None]
    unit_query = unit_rows(query_four.astype(jnp.float32))
    retrieved = jnp.einsum("rihd,rhde->rihe", unit_query, memory, precision=lax.Precision.HIGHEST)
    mixed = (attention + retrieved).reshape(group_rows, width).astype(jnp.bfloat16)
    rows = group_rows // lax.axis_size("grp")
    head_sum = lax.psum_scatter(
        jnp.dot(mixed, w_out, preferred_element_type=jnp.float32).astype(jnp.bfloat16),
        "grp",
        scatter_dimension=0,
        tiled=True,
    ).astype(jnp.float32)
    own_rows = lax.dynamic_slice_in_dim(tokens, lax.axis_index("grp") * rows, rows, 0)
    residual = (own_rows.astype(jnp.float32) + head_sum).astype(jnp.bfloat16)
    ffn_in = rms_norm(residual, norm_ffn)
    piece = lax.all_gather(ffn_in, "grp", axis=0, tiled=True)
    gate = jnp.dot(piece, w_gate_up[0], preferred_element_type=jnp.float32)
    up = jnp.dot(piece, w_gate_up[1], preferred_element_type=jnp.float32)
    hidden = (jax.nn.silu(gate) * up).astype(jnp.bfloat16)
    ffn_out = lax.psum_scatter(
        jnp.dot(hidden, w_down, preferred_element_type=jnp.float32).astype(jnp.bfloat16),
        "grp",
        scatter_dimension=0,
        tiled=True,
    ).astype(jnp.float32)
    layer_out = (residual.astype(jnp.float32) + ffn_out).astype(jnp.bfloat16)
    req_rows = request_ids[:, None]
    path_keys = unit_rows(key_four[req_rows, accept_path].astype(jnp.float32))
    path_values = value_four[req_rows, accept_path].astype(jnp.float32)
    eta = 0.97 - 0.06 * momentum_code.astype(jnp.float32)
    forget = 0.01 + 0.02 * forget_code.astype(jnp.float32)
    for step in range(accept_path.shape[1]):
        unit = path_keys[:, step]
        predicted = jnp.einsum("rhd,rhde->rhe", unit, memory, precision=lax.Precision.HIGHEST)
        grad = jnp.einsum(
            "rhd,rhe->rhde", unit, predicted - path_values[:, step], precision=lax.Precision.HIGHEST
        )
        new_mom = eta[:, step, :, None, None] * momentum - THETA * grad
        new_mem = (1.0 - forget[:, step, :, None, None]) * memory + new_mom
        live = (step < accept_len)[:, None, None, None]
        momentum = jnp.where(live, new_mom, momentum)
        memory = jnp.where(live, new_mem, memory)
    return (layer_out, memory, momentum)


def solution(mesh):
    return jax.shard_map(
        on_device,
        mesh=mesh,
        in_specs=(
            P("req", None),
            P(),
            P(None, "grp"),
            P(None, "grp"),
            P(None, "grp"),
            P("grp", None),
            P(None, "grp"),
            P(None, "grp"),
            P("req", None, None, "grp"),
            P("req"),
            P("req"),
            P("req"),
            P("req", None, None),
            P("req", None),
            P("req"),
            P("req", "grp", None, None),
            P("req", "grp", None, None),
            P("req", None, "grp"),
            P("req", None, "grp"),
            P(),
            P(None, None, "grp"),
            P("grp", None),
        ),
        out_specs=(
            P(("req", "grp"), None),
            P("req", "grp", None, None),
            P("req", "grp", None, None),
        ),
        check_vma=False,
    )
```

profile of v0, /device:TPU:0, one launch (start us, length us, event | category | flops | bytes accessed | tf_op | source)
XLA Modules:
  0.0 470.7 jit_solution(17253716148561162837)
XLA Ops:
  8.7 7.4 %all-to-all-start = ((s32[16,3,1]{1,2,0:T(1,128)}), s32[16,3,1]{1,2,0:T(1,128)S(1)}, u32[]{:S(2)}, u32[]{:S(2)}) async-start(s32[16,3,1]{1,2,0:T(1,128)} %bitcast.6), calls=%async_computation | async-start | bytes 16384 | tf_op jit(solution)/shard_map/all_to_all | solution.py:122
  17.4 5.0 %all-to-all-done = s32[16,3,1]{1,2,0:T(1,128)S(1)} async-done(((s32[16,3,1]{1,2,0:T(1,128)}), s32[16,3,1]{1,2,0:T(1,128)S(1)}, u32[]{:S(2)}, u32[]{:S(2)}) %all-to-all-start) | async-done | bytes 224 | tf_op jit(solution)/shard_map/all_to_all | solution.py:122
  22.4 3.5 all-to-all-start.1
  25.9 16.7 %copy.234 = bf16[48,2,128,512]{2,3,1,0:T(8,128)(2,1)} copy(bf16[48,2,128,512]{3,2,1,0:T(8,128)(2,1)} %param.30) | data formatting | bytes 25165824 | tf_op args[8]
  43.2 6.0 %all-to-all-start.2 = ((bf16[48,2,128,512]{2,3,1,0:T(8,128)(2,1)}), bf16[48,2,128,512]{2,3,1,0:T(8,128)(2,1)}, u32[]{:S(2)}, u32[]{:S(2)}) async-start(bf16[48,2,128,512]{2,3,1,0:T(8,128)(2,1)} %copy.234), calls=%async_computation.2 | async-start | bytes 25165824 | tf_op jit(solution)/shard_map/all_to_all | solution.py:121
  51.4 3.1 convolution_convert_fusion.4
  65.3 3.1 convolution_convert_fusion.2
  94.5 5.5 %fusion.145 = f32[16,4,1,128]{3,2,1,0:T(1,128)S(1)} fusion(f32[16,4,128,1]{2,3,1,0:T(1,128)S(1)} %bitcast.263, f32[16,4,128,128]{3,2,1,0:T(8,128)} %param.37), kind=kOutput, calls=%fused_computation.235 | convolution fusion | flops 12582912 | bytes 4259840 | tf_op jit(solution)/shard_map/rhd,rhde->rhe/dot_general | solution.py:180
  100.0 6.6 %fusion.36 = f32[16,4,1,128]{3,2,1,0:T(1,128)S(1)} fusion(f32[16,4,128,1]{2,3,1,0:T(1,128)S(1)} %bitcast.262, f32[16,4,128,128]{3,2,1,0:T(8,128)} %param.37, f32[16,4,128,128]{3,2,1,0:T(8,128)S(1)} %copy-done.1, f32[16,4,128]{2,1,0:T(4,128)S(1)} %fusion.104, f32[16,4,128]{2,1,0:T(4,128)S(1)} %get-tuple-element.14, f32[16,4]{1,0:T(8,128)S(1)} %copy.260, ...), kind=kOutput, calls=%fused_computation.61 | convolution fusion | flops 19922944 | bytes 8520208 | tf_op jit(solution)/shard_map/rhd,rhde->rhe/dot_general | solution.py:180
  106.7 3.6 add_select_fusion.6
  110.3 3.7 fusion.146
  114.0 7.9 %fusion.30 = f32[16,4,1,128]{3,2,1,0:T(1,128)S(1)} fusion(f32[16,4,128,1]{2,3,1,0:T(1,128)S(1)} %bitcast.272, f32[16,4,128,128]{3,2,1,0:T(8,128)S(1)} %add_select_fusion.6, f32[16,4,128]{2,1,0:T(4,128)S(1)} %fusion.102, f32[16,4,128]{2,1,0:T(4,128)S(1)} %get-tuple-element.16, f32[16,4]{1,0:T(8,128)S(1)} %copy-done.30, f32[16,4]{1,0:T(8,128)S(1)} %copy-done.50, ...), kind=kOutput, calls=%fused_computation.55 | convolution fusion | flops 30408704 | bytes 8651824 | tf_op jit(solution)/shard_map/rhd,rhde->rhe/dot_general | solution.py:180
  122.0 6.4 %add_select_fusion.4 = f32[16,4,128,128]{3,2,1,0:T(8,128)S(1)} fusion(f32[16,4,128]{2,1,0:T(4,128)S(1)} %fusion.101, f32[16,4,128]{2,1,0:T(4,128)S(1)} %get-tuple-element.17, f32[16,4]{1,0:T(8,128)S(1)} %copy-done.32, f32[16,4,128]{2,1,0:T(4,128)S(1)} %fusion.102, f32[16,4,128,128]{3,2,1,0:T(8,128)S(1)} %add_select_fusion.6, ...), kind=kLoop, calls=%fused_computation.17 | loop fusion | flops 26214400 | bytes 12846656 | tf_op jit(solution)/shard_map/jit(_where)/select_n | solution.py:188
  128.4 3.6 fusion.147
  134.2 5.7 %fusion.6 = f32[16,4,128,128]{3,2,1,0:T(8,128)S(1)} fusion(f32[16,4,128]{2,1,0:T(4,128)S(1)} %fusion.101, f32[16,4,128]{2,1,0:T(4,128)S(1)} %get-tuple-element.17, f32[16,4]{1,0:T(8,128)S(1)} %copy-done.32, f32[16,4,128]{2,1,0:T(4,128)S(1)} %fusion.102, f32[16,4,128]{2,1,0:T(4,128)S(1)} %get-tuple-element.16, f32[16,4]{1,0:T(8,128)S(1)} %copy-done.30, ...), kind=kLoop, calls=%fused_computation.19 | loop fusion | flops 20971520 | bytes 8651840 | tf_op jit(solution)/shard_map/jit(_where)/select_n | solution.py:187
  142.0 4.9 %fusion.27 = f32[16,4,1,128]{3,2,1,0:T(1,128)} fusion(f32[16,4,128,1]{2,3,1,0:T(1,128)S(1)} %bitcast.259, f32[16,4,128,128]{3,2,1,0:T(8,128)S(1)} %add_select_fusion.4, f32[16,4,128,128]{3,2,1,0:T(8,128)S(1)} %fusion.6, f32[16,4,128]{2,1,0:T(4,128)S(1)} %fusion.100, f32[16,4,128]{2,1,0:T(4,128)S(1)} %get-tuple-element.18, f32[16,4]{1,0:T(8,128)S(1)} %copy-done.36, ...), kind=kOutput, calls=%fused_computation.52 | convolution fusion | flops 19922944 | bytes 8520208 | tf_op jit(solution)/shard_map/rhd,rhde->rhe/dot_general | solution.py:180
  161.5 111.4 %all-to-all-done.2 = bf16[48,2,128,512]{2,3,1,0:T(8,128)(2,1)} async-done(((bf16[48,2,128,512]{2,3,1,0:T(8,128)(2,1)}), bf16[48,2,128,512]{2,3,1,0:T(8,128)(2,1)}, u32[]{:S(2)}, u32[]{:S(2)}) %all-to-all-start.2) | async-done | bytes 12582944 | tf_op jit(solution)/shard_map/all_to_all | solution.py:121
  272.9 8.6 %fusion.142 = (bf16[48,1,128,512]{2,3,1,0:T(8,128)(2,1)}, bf16[48,1,128,512]{2,3,1,0:T(8,128)(2,1)S(1)}) fusion(bf16[48,2,128,512]{2,3,1,0:T(8,128)(2,1)} %all-to-all-done.2), kind=kLoop, calls=%fused_computation.232 | loop fusion | bytes 25165824 | tf_op jit(solution)/shard_map/slice | solution.py:31
  281.6 4.1 fusion.18
  293.7 4.6 fusion.19
  298.3 5.9 %bitcast_multiply_fusion = f32[48,32,4,128]{3,1,2,0:T(8,128)S(1)} fusion(bf16[48,128,4,128]{1,3,2,0:T(8,128)(2,1)} %bitcast.250, f32[48,4,32,128]{3,2,1,0:T(8,128)S(1)} %copy-done.6, f32[48,32,4]{1,2,0:T(4,128)} %copy.244, f32[48,4,32]{2,1,0:T(4,128)} %get-tuple-element.53, pred[48,128]{1,0:T(8,128)(4,1)} %add_compare_fusion), kind=kOutput, calls=%fused_computation.30 | convolution fusion | flops 206045184 | bytes 12638208 | tf_op jit(solution)/shard_map/shit,sthd->sihd/dot_general | solution.py:42
  304.3 4.7 fusion.10
  316.3 3.9 fusion.70
  325.9 10.3 %add_select_fusion.2 = f32[16,4,128,128]{3,2,1,0:T(8,128)S(1)} fusion(f32[16,4,128]{2,1,0:T(4,128)S(1)} %fusion.99, f32[16,4,128]{2,1,0:T(4,128)S(1)} %copy-done.26, f32[16,4]{1,0:T(8,128)S(1)} %copy.271, f32[16,4,128]{2,1,0:T(4,128)S(1)} %copy-done.22, f32[16,4,128,128]{3,2,1,0:T(8,128)} %copy-done.4, f32[16,4,128]{2,1,0:T(4,128)S(1)} %copy-done.20, ...), kind=kLoop, calls=%fused_computation.11 | loop fusion | flops 36700160 | bytes 12978272 | tf_op jit(solution)/shard_map/jit(_where)/select_n | solution.py:188
  338.3 3.7 fusion.148
  343.3 48.5 %reduce-scatter.3.cloned.1.call-done = bf16[256,1024]{1,0:T(8,128)(2,1)} async-done(((bf16[512,1024]{1,0:T(8,128)(2,1)}), bf16[256,1024]{1,0:T(8,128)(2,1)}) %reduce-scatter.3.cloned.1.call-update) | async-done | bytes 524304 | tf_op jit(solution)/shard_map/reduce_scatter | solution.py:153
  395.0 9.2 %fusion.24 = f32[16,4,1,128]{3,2,1,0:T(1,128)S(1)} fusion(f32[16,4,128,1]{2,3,1,0:T(1,128)} %bitcast.271, f32[16,4,128,128]{3,2,1,0:T(8,128)} %copy-done.5, f32[16,4,128]{2,1,0:T(4,128)} %fusion.98, f32[16,4,128]{2,1,0:T(4,128)} %get-tuple-element.20, f32[16,4]{1,0:T(8,128)} %copy.273, f32[16,4]{1,0:T(8,128)} %copy.253, ...), kind=kOutput, calls=%fused_computation.49 | convolution fusion | flops 30408704 | bytes 8651824 | tf_op jit(solution)/shard_map/rhd,rhde->rhe/dot_general | solution.py:180
  405.6 11.0 %all-gather.2.cloned.1.call-done = bf16[512,1024]{1,0:T(8,128)(2,1)} async-done(((bf16[256,1024]{1,0:T(8,128)(2,1)}), bf16[512,1024]{1,0:T(8,128)(2,1)}) %all-gather.2.cloned.1.call-update) | async-done | bytes 1048592 | tf_op jit(solution)/shard_map/all_gather | solution.py:162
  416.6 5.5 %fusion.14 = f32[512,1408]{1,0:T(8,128)} fusion(bf16[512,1024]{1,0:T(8,128)(2,1)} %all-gather.2.cloned.1.call-done, bf16[2,1024,1408]{2,1,0:T(8,128)(2,1)} %param.42), kind=kOutput, calls=%fused_computation.37 | convolution fusion | flops 1476395008 | bytes 6815744 | tf_op jit(solution)/shard_map/dot_general | solution.py:163
  422.1 7.4 %convolution_convert_fusion = bf16[512,1024]{1,0:T(8,128)(2,1)} fusion(bf16[1408,1024]{1,0:T(8,128)(2,1)S(1)} %copy-done, bf16[512,1024]{1,0:T(8,128)(2,1)} %all-gather.2.cloned.1.call-done, bf16[2,1024,1408]{2,1,0:T(8,128)(2,1)} %param.42, f32[512,1408]{1,0:T(8,128)} %fusion.14), kind=kOutput, calls=%fused_computation.84 | convolution fusion | flops 2957639680 | bytes 10747904 | tf_op jit(solution)/shard_map/dot_general | solution.py:167
  429.6 15.2 %fusion.2 = f32[16,4,128,128]{3,2,1,0:T(8,128)} fusion(f32[16,4,128]{2,1,0:T(4,128)} %fusion.97, f32[16,4,128]{2,1,0:T(4,128)} %get-tuple-element.13, f32[16,4]{1,0:T(8,128)} %copy.275, f32[16,4,128]{2,1,0:T(4,128)} %fusion.98, f32[16,4,128]{2,1,0:T(4,128)} %get-tuple-element.20, f32[16,4]{1,0:T(8,128)} %copy.273, pred[16]{0:T(512)(128)(4,1)} %get-tuple-element.50, ...), kind=kLoop, calls=%fused_computation.7 | loop fusion | flops 41943040 | bytes 8915072 | tf_op jit(solution)/shard_map/jit(_where)/select_n | solution.py:187
  446.1 15.8 %add_select_fusion = f32[16,4,128,128]{3,2,1,0:T(8,128)} fusion(f32[16,4,128]{2,1,0:T(4,128)} %fusion.97, f32[16,4,128]{2,1,0:T(4,128)} %get-tuple-element.13, f32[16,4]{1,0:T(8,128)} %copy.275, f32[16,4,128]{2,1,0:T(4,128)} %fusion.98, f32[16,4,128,128]{3,2,1,0:T(8,128)} %copy-done.5, f32[16,4,128]{2,1,0:T(4,128)} %get-tuple-element.20, f32[16,4]{1,0:T(8,128)} %copy.273, ...), kind=kLoop, calls=%fused_computation.5 | loop fusion | flops 47185920 | bytes 13109888 | tf_op jit(solution)/shard_map/jit(_where)/select_n | solution.py:188
  (234 shorter events, 93.2 us)
Async XLA Ops:
  7.2 414.9 %copy-start = (bf16[1408,1024]{1,0:T(8,128)(2,1)S(1)}, bf16[1408,1024]{1,0:T(8,128)(2,1)}, u32[]{:S(2)}) copy-start(bf16[1408,1024]{1,0:T(8,128)(2,1)} %param.43) | copy-start | bytes 8650756
  8.7 13.7 %all-to-all-start = ((s32[16,3,1]{1,2,0:T(1,128)}), s32[16,3,1]{1,2,0:T(1,128)S(1)}, u32[]{:S(2)}, u32[]{:S(2)}) async-start(s32[16,3,1]{1,2,0:T(1,128)} %bitcast.6), calls=%async_computation | async-start | bytes 16384 | tf_op jit(solution)/shard_map/all_to_all | solution.py:122
  22.4 20.1 %copy-start.48 = (s32[16,3,1]{1,2,0:T(1,128)}, s32[16,3,1]{1,2,0:T(1,128)S(1)}, u32[]{:S(2)}) copy-start(s32[16,3,1]{1,2,0:T(1,128)S(1)} %all-to-all-done) | copy-start | bytes 580
  22.4 20.2 %all-to-all-start.1 = ((s32[16,3,1]{1,2,0:T(1,128)}), s32[16,3,1]{1,2,0:T(1,128)S(1)}, u32[]{:S(2)}, u32[]{:S(2)}) async-start(s32[16,3,1]{1,2,0:T(1,128)} %bitcast.7), calls=%async_computation.1 | async-start | bytes 16384 | tf_op jit(solution)/shard_map/all_to_all | solution.py:123
  42.6 8.8 %copy-start.70 = (f32[1024]{0:T(1024)S(1)}, f32[1024]{0:T(1024)}, u32[]{:S(2)}) copy-start(f32[1024]{0:T(1024)} %param.23) | copy-start | bytes 12292
  43.2 229.8 %all-to-all-start.2 = ((bf16[48,2,128,512]{2,3,1,0:T(8,128)(2,1)}), bf16[48,2,128,512]{2,3,1,0:T(8,128)(2,1)}, u32[]{:S(2)}, u32[]{:S(2)}) async-start(bf16[48,2,128,512]{2,3,1,0:T(8,128)(2,1)} %copy.234), calls=%async_computation.2 | async-start | bytes 25165824 | tf_op jit(solution)/shard_map/all_to_all | solution.py:121
  49.2 342.6 %reduce-scatter.3.cloned.1.call-start = ((), (), s32[]{:S(2)}) async-start(), calls=%async_computation.5 | async-start | bytes 1572864 | tf_op jit(solution)/shard_map/reduce_scatter | solution.py:153
  58.8 11.6 %copy-start.68 = (s32[16,8]{0,1:T(8,128)S(1)}, s32[16,8]{0,1:T(8,128)}, u32[]{:S(2)}) copy-start(s32[16,8]{0,1:T(8,128)} %param.35) | copy-start | bytes 1540
  90.8 9.2 %copy-start.18 = (f32[16,8,4,128]{3,2,1,0:T(4,128)S(1)}, f32[16,8,4,128]{3,2,1,0:T(4,128)}, u32[]{:S(2)}) copy-start(f32[16,8,4,128]{3,2,1,0:T(4,128)} %convert.1) | copy-start | bytes 786436
  90.8 9.2 %copy-start.1 = (f32[16,4,128,128]{3,2,1,0:T(8,128)S(1)}, f32[16,4,128,128]{3,2,1,0:T(8,128)}, u32[]{:S(2)}) copy-start(f32[16,4,128,128]{3,2,1,0:T(8,128)} %param.38) | copy-start | bytes 12582916
  90.8 9.2 %copy-start.44 = (f32[16,4]{1,0:T(8,128)S(1)}, f32[16,4]{1,0:T(8,128)}, u32[]{:S(2)}) copy-start(f32[16,4]{1,0:T(8,128)} %copy.259) | copy-start | bytes 772
  92.9 41.3 %copy-start.52 = (pred[16]{0:T(512)(128)(4,1)}, pred[16]{0:T(512)(128)(4,1)S(1)}, u32[]{:S(2)}) copy-start(pred[16]{0:T(512)(128)(4,1)S(1)} %get-tuple-element.52) | copy-start | bytes 52
  92.9 41.3 %copy-start.54 = (pred[16]{0:T(512)(128)(4,1)}, pred[16]{0:T(512)(128)(4,1)S(1)}, u32[]{:S(2)}) copy-start(pred[16]{0:T(512)(128)(4,1)S(1)} %get-tuple-element.46) | copy-start | bytes 52
  92.9 41.3 %copy-start.56 = (pred[16]{0:T(512)(128)(4,1)}, pred[16]{0:T(512)(128)(4,1)S(1)}, u32[]{:S(2)}) copy-start(pred[16]{0:T(512)(128)(4,1)S(1)} %get-tuple-element.47) | copy-start | bytes 52
  92.9 47.1 %copy-start.60 = (pred[16]{0:T(512)(128)(4,1)}, pred[16]{0:T(512)(128)(4,1)S(1)}, u32[]{:S(2)}) copy-start(pred[16]{0:T(512)(128)(4,1)S(1)} %get-tuple-element.48) | copy-start | bytes 52
  94.5 39.7 %copy-start.9 = (f32[16,4,128]{2,1,0:T(4,128)}, f32[16,4,128]{2,1,0:T(4,128)S(1)}, u32[]{:S(2)}) copy-start(f32[16,4,128]{2,1,0:T(4,128)S(1)} %get-tuple-element.16) | copy-start | bytes 98308
  94.5 39.7 %copy-start.11 = (f32[16,4,128]{2,1,0:T(4,128)}, f32[16,4,128]{2,1,0:T(4,128)S(1)}, u32[]{:S(2)}) copy-start(f32[16,4,128]{2,1,0:T(4,128)S(1)} %get-tuple-element.17) | copy-start | bytes 98308
  94.5 45.5 %copy-start.19 = (f32[16,4,128]{2,1,0:T(4,128)}, f32[16,4,128]{2,1,0:T(4,128)S(1)}, u32[]{:S(2)}) copy-start(f32[16,4,128]{2,1,0:T(4,128)S(1)} %get-tuple-element.18) | copy-start | bytes 98308
  113.9 20.2 %copy-start.13 = (f32[16,4,128]{2,1,0:T(4,128)}, f32[16,4,128]{2,1,0:T(4,128)S(1)}, u32[]{:S(2)}) copy-start(f32[16,4,128]{2,1,0:T(4,128)S(1)} %fusion.102) | copy-start | bytes 98308
  114.0 8.0 %copy-start.32 = (f32[16,4]{1,0:T(8,128)S(1)}, f32[16,4]{1,0:T(8,128)}, u32[]{:S(2)}) copy-start(f32[16,4]{1,0:T(8,128)} %copy.267) | copy-start | bytes 772
  114.0 8.0 %copy-start.51 = (f32[16,4]{1,0:T(8,128)S(1)}, f32[16,4]{1,0:T(8,128)}, u32[]{:S(2)}) copy-start(f32[16,4]{1,0:T(8,128)} %copy.256) | copy-start | bytes 772
  122.0 12.2 %copy-start.15 = (f32[16,4,128]{2,1,0:T(4,128)}, f32[16,4,128]{2,1,0:T(4,128)S(1)}, u32[]{:S(2)}) copy-start(f32[16,4,128]{2,1,0:T(4,128)S(1)} %fusion.101) | copy-start | bytes 98308
  128.4 11.6 %copy-start.4 = (f32[16,4,128,128]{3,2,1,0:T(8,128)}, f32[16,4,128,128]{3,2,1,0:T(8,128)S(1)}, u32[]{:S(2)}) copy-start(f32[16,4,128,128]{3,2,1,0:T(8,128)S(1)} %add_select_fusion.4) | copy-start | bytes 12582916
  132.1 7.9 %copy-start.21 = (f32[16,4,128]{2,1,0:T(4,128)}, f32[16,4,128]{2,1,0:T(4,128)S(1)}, u32[]{:S(2)}) copy-start(f32[16,4,128]{2,1,0:T(4,128)S(1)} %fusion.100) | copy-start | bytes 98308
  134.2 7.8 %copy-start.36 = (f32[16,4]{1,0:T(8,128)S(1)}, f32[16,4]{1,0:T(8,128)}, u32[]{:S(2)}) copy-start(f32[16,4]{1,0:T(8,128)} %copy.269) | copy-start | bytes 772
  272.9 8.6 %copy-start.8 = (bf16[48,32,512]{2,1,0:T(8,128)(2,1)S(1)}, bf16[48,32,512]{2,1,0:T(8,128)(2,1)}, u32[]{:S(2)}) copy-start(bf16[48,32,512]{2,1,0:T(8,128)(2,1)} %gather_fusion) | copy-start | bytes 4718596
  272.9 8.6 %copy-start.43 = (pred[48,128]{1,0:T(8,128)(4,1)S(1)}, pred[48,128]{1,0:T(8,128)(4,1)}, u32[]{:S(2)}) copy-start(pred[48,128]{1,0:T(8,128)(4,1)} %add_compare_fusion) | copy-start | bytes 18436
  322.7 93.9 %all-gather.2.cloned.1.call-start = ((), (), s32[]{:S(2)}) async-start(), calls=%async_computation.6 | async-start | bytes 1572864 | tf_op jit(solution)/shard_map/all_gather | solution.py:162
  323.5 12.7 %copy-start.27 = (f32[16,4,128]{2,1,0:T(4,128)}, f32[16,4,128]{2,1,0:T(4,128)S(1)}, u32[]{:S(2)}) copy-start(f32[16,4,128]{2,1,0:T(4,128)S(1)} %fusion.99) | copy-start | bytes 98308
  323.6 12.6 %copy-start.42 = (f32[16,4]{1,0:T(8,128)}, f32[16,4]{1,0:T(8,128)S(1)}, u32[]{:S(2)}) copy-start(f32[16,4]{1,0:T(8,128)S(1)} %copy.271) | copy-start | bytes 772
  325.9 12.4 %copy-start.38 = (f32[16,1,4,128]{3,2,1,0:T(4,128)S(1)}, f32[16,1,4,128]{3,2,1,0:T(4,128)}, u32[]{:S(2)}) copy-start(f32[16,1,4,128]{3,2,1,0:T(4,128)} %get-tuple-element.22) | copy-start | bytes 98308
  395.0 66.9 %reduce-scatter.5.cloned.1.call-start = ((), (), s32[]{:S(2)}) async-start(), calls=%async_computation.7 | async-start | bytes 1572864 | tf_op jit(solution)/shard_map/reduce_scatter | solution.py:166
  (45 other events, 209.1 us)
Sparse Core Ops, SparseCore 0:
  322.8 68.9 reduce-scatter.2
  395.1 21.4 all-gather.1
  429.7 20.3 reduce-scatter.4
where the time goes:
time: 478 us; the launch traced here: 471 us
  waiting for transfers between devices  176 us (37%)
  matrix products  96.6 us (20%)
  other arithmetic  91.4 us (19%)
  local copies, waits for them, and re-layouts  74.8 us (16%)
  starting transfers between devices  17 us (4%)
  between operations  15 us (3%)
    all_to_all x1, waiting for transfers between devices, on_device(): lax.all_to_all(kv_cache, 'req', split_axis=0, concat_axis=0, tiled=True)  111 us
    reduce_scatter x1, waiting for transfers between devices, on_device(): lax.psum_scatter(jnp.dot(mixed, w_out, preferred_element_type=jnp.float32...  48.5 us
    dot_general x8, matrix products, on_device(): jnp.einsum('rhd,rhde->rhe', unit, memory, precision=lax.Precision.HIGHEST)  45.1 us
    select_n x4, other arithmetic, on_device(): memory = jnp.where(live, new_mem, memory)  36 us
    unnamed x143, local copies, waits for them, and re-layouts  21.6 us
    select_n x2, other arithmetic, on_device(): momentum = jnp.where(live, new_mom, momentum)  20.9 us
    all_gather x1, waiting for transfers between devices, on_device(): piece = lax.all_gather(ffn_in, 'grp', axis=0, tiled=True)  11 us
  transfers between devices with their start and end apart: 6, of which 4 were waited for; matrix products, arithmetic and copies ran while one was open for 40% of the time, Pallas kernels for 0%

commit v1 on v0

--- a/solution.py
+++ b/solution.py
@@ -8,6 +8,35 @@
 EPS = 1e-06
 THETA = 0.5
 NEG = -1e30
+
+
+def write_target(inner_x, on_dim, piece_in):
+    t1 = inner_x.shape
+    arr_out = inner_x.reshape(*t1[:on_dim], piece_in, t1[on_dim] // piece_in, *t1[on_dim + 1 :])
+    return jnp.moveaxis(arr_out, on_dim, 0)
+
+
+def set_core(x_part, at_axis):
+    x_part = jnp.moveaxis(x_part, 0, at_axis)
+    local_now = x_part.shape
+    return x_part.reshape(
+        *local_now[:at_axis], local_now[at_axis] * local_now[at_axis + 1], *local_now[at_axis + 2 :]
+    )
+
+
+def _unite_slot(local_block, row_data, axis_tag, a0):
+    oldest, now = (lax.axis_size(axis_tag), lax.axis_index(axis_tag))
+    k_now = write_target(a0, row_data, oldest)
+    s = 1
+    entries = [k_now[now]]
+    while s < oldest:
+        upper = k_now[now ^ s]
+        entries.append(
+            lax.ppermute(upper, axis_name=axis_tag, perm=[(u, u ^ s) for u in range(oldest)])
+        )
+        s += 1
+    k_now = jnp.stack(entries, axis=0)[now ^ jnp.arange(oldest)]
+    return set_core(k_now, local_block)
 
 
 def rms_norm(rows, gain):
@@ -119,7 +148,7 @@
     request_ids = jnp.arange(reqs, dtype=jnp.int32)
     moved_pages, moved_request, moved_page = (
         lax.all_to_all(kv_cache, "req", split_axis=0, concat_axis=0, tiled=True),
-        lax.all_to_all(slot_request, "req", split_axis=0, concat_axis=0, tiled=True),
+        _unite_slot(0, 0, "req", slot_request),
         lax.all_to_all(slot_page, "req", split_axis=0, concat_axis=0, tiled=True),
     )
     local_request = moved_request - first_request

time: 478 us -> 490 us (1.025)
  starting transfers between devices: 17 us -> 36.6 us
    ppermute x0 -> x15, waiting for transfers between devices: none -> 163 us  [_unite_slot(): lax.ppermute(upper, axis_name=axis_tag, perm=[(u, u ^ s) for u in range(o...]
    all_to_all x1, waiting for transfers between devices: 111 us -> 0.01 us  [on_device(): lax.all_to_all(kv_cache, 'req', split_axis=0, concat_axis=0, tiled=True)]
    reduce_scatter x1, waiting for transfers between devices: 48.5 us -> 0.01 us  [on_device(): lax.psum_scatter(jnp.dot(mixed, w_out, preferred_element_type=jnp.float32...]
    ppermute x0 -> x15, starting transfers between devices: none -> 23 us  [_unite_slot(): lax.ppermute(upper, axis_name=axis_tag, perm=[(u, u ^ s) for u in range(o...]
    all_to_all x1 -> x0, starting transfers between devices: 7.39 us -> none  [on_device(): lax.all_to_all(slot_request, 'req', split_axis=0, concat_axis=0, tiled=True)]
    all_to_all x1 -> x0, waiting for transfers between devices: 4.99 us -> none  [on_device(): lax.all_to_all(slot_request, 'req', split_axis=0, concat_axis=0, tiled=True)]
    unnamed x143 -> x185, local copies, waits for them, and re-layouts: 21.6 us -> 20.1 us
  transfers between devices with their start and end apart: 6 -> 20, of which waited for: 4 -> 5; matrix products, arithmetic and copies ran while one was open for 40% -> 38% of each run, Pallas kernels for 0% -> 0%
where the time goes in v1:
time: 490 us; the launch traced here: 482 us
  waiting for transfers between devices  173 us (35%)
  matrix products  96.6 us (20%)
  other arithmetic  87.9 us (18%)
  local copies, waits for them, and re-layouts  73 us (15%)
  starting transfers between devices  36.6 us (7%)
  between operations  15.4 us (3%)
    ppermute x15, waiting for transfers between devices, _unite_slot(): lax.ppermute(upper, axis_name=axis_tag, perm=[(u, u ^ s) for u in range(o...  163 us
    dot_general x8, matrix products, on_device(): jnp.einsum('rhd,rhde->rhe', unit, memory, precision=lax.Precision.HIGHEST)  45.1 us
    select_n x4, other arithmetic, on_device(): memory = jnp.where(live, new_mem, memory)  36 us
    ppermute x15, starting transfers between devices, _unite_slot(): lax.ppermute(upper, axis_name=axis_tag, perm=[(u, u ^ s) for u in range(o...  23 us
    select_n x2, other arithmetic, on_device(): momentum = jnp.where(live, new_mom, momentum)  20.9 us
    unnamed x185, local copies, waits for them, and re-layouts  20.1 us
  transfers between devices with their start and end apart: 20, of which 5 were waited for; matrix products, arithmetic and copies ran while one was open for 38% of the time, Pallas kernels for 0%

profile of v1, /device:TPU:0, one launch (start us, length us, event | category | flops | bytes accessed | tf_op | source)
XLA Modules:
  0.0 482.1 jit_solution(10953448743270184360)
XLA Ops:
  8.7 7.4 %all-to-all-start = ((s32[16,3,1]{1,2,0:T(1,128)}), s32[16,3,1]{1,2,0:T(1,128)S(1)}, u32[]{:S(2)}, u32[]{:S(2)}) async-start(s32[16,3,1]{1,2,0:T(1,128)} %bitcast.37), calls=%async_computation | async-start | bytes 16384 | tf_op jit(solution)/shard_map/all_to_all | solution.py:152
  16.1 16.7 %copy.265 = bf16[48,2,128,512]{2,3,1,0:T(8,128)(2,1)} copy(bf16[48,2,128,512]{3,2,1,0:T(8,128)(2,1)} %param.30) | data formatting | bytes 25165824 | tf_op args[8]
  33.3 6.0 %all-to-all-start.1 = ((bf16[48,2,128,512]{2,3,1,0:T(8,128)(2,1)}), bf16[48,2,128,512]{2,3,1,0:T(8,128)(2,1)}, u32[]{:S(2)}, u32[]{:S(2)}) async-start(bf16[48,2,128,512]{2,3,1,0:T(8,128)(2,1)} %copy.265), calls=%async_computation.1 | async-start | bytes 25165824 | tf_op jit(solution)/shard_map/all_to_all | solution.py:150
  46.4 3.1 convolution_convert_fusion.4
  50.7 3.1 convolution_convert_fusion.3
  89.7 5.5 %fusion.160 = f32[16,4,1,128]{3,2,1,0:T(1,128)S(1)} fusion(f32[16,4,128,1]{2,3,1,0:T(1,128)S(1)} %bitcast.307, f32[16,4,128,128]{3,2,1,0:T(8,128)} %param.37), kind=kOutput, calls=%fused_computation.269 | convolution fusion | flops 12582912 | bytes 4259840 | tf_op jit(solution)/shard_map/rhd,rhde->rhe/dot_general | solution.py:209
  95.2 6.6 %fusion.36 = f32[16,4,1,128]{3,2,1,0:T(1,128)S(1)} fusion(f32[16,4,128,1]{2,3,1,0:T(1,128)S(1)} %bitcast.306, f32[16,4,128,128]{3,2,1,0:T(8,128)} %param.37, f32[16,4,128,128]{3,2,1,0:T(8,128)S(1)} %copy-done.1, f32[16,4,128]{2,1,0:T(4,128)S(1)} %fusion.104, f32[16,4,128]{2,1,0:T(4,128)S(1)} %get-tuple-element.12, f32[16,4]{1,0:T(8,128)S(1)} %copy.291, ...), kind=kOutput, calls=%fused_computation.62 | convolution fusion | flops 19922944 | bytes 8520208 | tf_op jit(solution)/shard_map/rhd,rhde->rhe/dot_general | solution.py:209
  101.9 3.6 add_select_fusion.6
  105.5 3.7 fusion.161
  109.2 7.9 %fusion.30 = f32[16,4,1,128]{3,2,1,0:T(1,128)S(1)} fusion(f32[16,4,128,1]{2,3,1,0:T(1,128)S(1)} %bitcast.316, f32[16,4,128,128]{3,2,1,0:T(8,128)S(1)} %add_select_fusion.6, f32[16,4,128]{2,1,0:T(4,128)S(1)} %fusion.102, f32[16,4,128]{2,1,0:T(4,128)S(1)} %get-tuple-element.14, f32[16,4]{1,0:T(8,128)S(1)} %copy-done.32, f32[16,4]{1,0:T(8,128)S(1)} %copy-done.50, ...), kind=kOutput, calls=%fused_computation.56 | convolution fusion | flops 30408704 | bytes 8651824 | tf_op jit(solution)/shard_map/rhd,rhde->rhe/dot_general | solution.py:209
  117.2 6.4 %add_select_fusion.4 = f32[16,4,128,128]{3,2,1,0:T(8,128)S(1)} fusion(f32[16,4,128]{2,1,0:T(4,128)S(1)} %fusion.101, f32[16,4,128]{2,1,0:T(4,128)S(1)} %get-tuple-element.15, f32[16,4]{1,0:T(8,128)S(1)} %copy-done.34, f32[16,4,128]{2,1,0:T(4,128)S(1)} %fusion.102, f32[16,4,128,128]{3,2,1,0:T(8,128)S(1)} %add_select_fusion.6, ...), kind=kLoop, calls=%fused_computation.18 | loop fusion | flops 26214400 | bytes 12846656 | tf_op jit(solution)/shard_map/jit(_where)/select_n | solution.py:217
  123.7 3.6 fusion.162
  129.5 5.7 %fusion.6 = f32[16,4,128,128]{3,2,1,0:T(8,128)S(1)} fusion(f32[16,4,128]{2,1,0:T(4,128)S(1)} %fusion.101, f32[16,4,128]{2,1,0:T(4,128)S(1)} %get-tuple-element.15, f32[16,4]{1,0:T(8,128)S(1)} %copy-done.34, f32[16,4,128]{2,1,0:T(4,128)S(1)} %fusion.102, f32[16,4,128]{2,1,0:T(4,128)S(1)} %get-tuple-element.14, f32[16,4]{1,0:T(8,128)S(1)} %copy-done.32, ...), kind=kLoop, calls=%fused_computation.20 | loop fusion | flops 20971520 | bytes 8651840 | tf_op jit(solution)/shard_map/jit(_where)/select_n | solution.py:216
  135.4 4.9 %fusion.27 = f32[16,4,1,128]{3,2,1,0:T(1,128)} fusion(f32[16,4,128,1]{2,3,1,0:T(1,128)S(1)} %bitcast.303, f32[16,4,128,128]{3,2,1,0:T(8,128)S(1)} %add_select_fusion.4, f32[16,4,128,128]{3,2,1,0:T(8,128)S(1)} %fusion.6, f32[16,4,128]{2,1,0:T(4,128)S(1)} %fusion.100, f32[16,4,128]{2,1,0:T(4,128)S(1)} %get-tuple-element.16, f32[16,4]{1,0:T(8,128)S(1)} %copy-done.38, ...), kind=kOutput, calls=%fused_computation.53 | convolution fusion | flops 19922944 | bytes 8520208 | tf_op jit(solution)/shard_map/rhd,rhde->rhe/dot_general | solution.py:209
  145.6 97.3 %collective-permute-done.3 = s32[3]{0:T(128)} collective-permute-done((s32[3]{0:T(128)}, s32[3]{0:T(128)}, u32[]{:S(2)}, u32[]{:S(2)}) %collective-permute-start.3) | collective-permute-done | bytes 44 | tf_op jit(solution)/shard_map/ppermute | solution.py:35
  242.9 3.7 collective-permute-start.8
  251.2 62.1 %collective-permute-done.7 = s32[3]{0:T(128)S(1)} collective-permute-done((s32[3]{0:T(128)S(1)}, s32[3]{0:T(128)S(1)}, u32[]{:S(2)}, u32[]{:S(2)}) %collective-permute-start.7) | collective-permute-done | bytes 44 | tf_op jit(solution)/shard_map/ppermute | solution.py:35
  313.6 3.4 collective-permute-start.13
  334.7 8.8 %fusion.157 = (bf16[48,1,128,512]{2,3,1,0:T(8,128)(2,1)}, bf16[48,1,128,512]{2,3,1,0:T(8,128)(2,1)S(1)}) fusion(bf16[48,2,128,512]{2,3,1,0:T(8,128)(2,1)} %all-to-all-done.1), kind=kLoop, calls=%fused_computation.266 | loop fusion | bytes 25165824 | tf_op jit(solution)/shard_map/slice | solution.py:60
  343.5 4.1 fusion.18
  355.7 4.1 fusion.19
  359.8 5.9 %bitcast_multiply_fusion = f32[48,32,4,128]{3,1,2,0:T(8,128)S(1)} fusion(bf16[48,128,4,128]{1,3,2,0:T(8,128)(2,1)} %bitcast.294, f32[48,4,32,128]{3,2,1,0:T(8,128)S(1)} %copy-done.6, f32[48,32,4]{1,2,0:T(4,128)} %copy.275, f32[48,4,32]{2,1,0:T(4,128)} %get-tuple-element.67, pred[48,128]{1,0:T(8,128)(4,1)S(1)} %add_compare_fusion), kind=kOutput, calls=%fused_computation.31 | convolution fusion | flops 206045184 | bytes 12638208 | tf_op jit(solution)/shard_map/shit,sthd->sihd/dot_general | solution.py:71
  365.7 4.7 fusion.10
  377.8 3.9 fusion.70
  387.3 10.3 %add_select_fusion.2 = f32[16,4,128,128]{3,2,1,0:T(8,128)S(1)} fusion(f32[16,4,128]{2,1,0:T(4,128)S(1)} %fusion.99, f32[16,4,128]{2,1,0:T(4,128)S(1)} %copy-done.26, f32[16,4]{1,0:T(8,128)S(1)} %copy.302, f32[16,4,128]{2,1,0:T(4,128)S(1)} %copy-done.22, f32[16,4,128,128]{3,2,1,0:T(8,128)} %copy-done.4, f32[16,4,128]{2,1,0:T(4,128)S(1)} %copy-done.20, ...), kind=kLoop, calls=%fused_computation.12 | loop fusion | flops 36700160 | bytes 12978272 | tf_op jit(solution)/shard_map/jit(_where)/select_n | solution.py:217
  399.7 3.7 fusion.163
  408.0 9.2 %fusion.24 = f32[16,4,1,128]{3,2,1,0:T(1,128)S(1)} fusion(f32[16,4,128,1]{2,3,1,0:T(1,128)} %bitcast.315, f32[16,4,128,128]{3,2,1,0:T(8,128)} %copy-done.5, f32[16,4,128]{2,1,0:T(4,128)} %fusion.98, f32[16,4,128]{2,1,0:T(4,128)} %get-tuple-element.18, f32[16,4]{1,0:T(8,128)} %copy.304, f32[16,4]{1,0:T(8,128)} %copy.284, ...), kind=kOutput, calls=%fused_computation.50 | convolution fusion | flops 30408704 | bytes 8651824 | tf_op jit(solution)/shard_map/rhd,rhde->rhe/dot_general | solution.py:209
  418.6 9.4 %all-gather.2.cloned.1.call-done = bf16[512,1024]{1,0:T(8,128)(2,1)} async-done(((bf16[256,1024]{1,0:T(8,128)(2,1)}), bf16[512,1024]{1,0:T(8,128)(2,1)}) %all-gather.2.cloned.1.call-update) | async-done | bytes 1048592 | tf_op jit(solution)/shard_map/all_gather | solution.py:191
  428.0 5.5 %fusion.14 = f32[512,1408]{1,0:T(8,128)} fusion(bf16[512,1024]{1,0:T(8,128)(2,1)} %all-gather.2.cloned.1.call-done, bf16[2,1024,1408]{2,1,0:T(8,128)(2,1)} %param.42), kind=kOutput, calls=%fused_computation.38 | convolution fusion | flops 1476395008 | bytes 6815744 | tf_op jit(solution)/shard_map/dot_general | solution.py:192
  433.5 7.4 %convolution_convert_fusion = bf16[512,1024]{1,0:T(8,128)(2,1)} fusion(bf16[1408,1024]{1,0:T(8,128)(2,1)S(1)} %copy-done, bf16[512,1024]{1,0:T(8,128)(2,1)} %all-gather.2.cloned.1.call-done, bf16[2,1024,1408]{2,1,0:T(8,128)(2,1)} %param.42, f32[512,1408]{1,0:T(8,128)} %fusion.14), kind=kOutput, calls=%fused_computation.85 | convolution fusion | flops 2957639680 | bytes 10747904 | tf_op jit(solution)/shard_map/dot_general | solution.py:196
  441.0 15.2 %fusion.2 = f32[16,4,128,128]{3,2,1,0:T(8,128)} fusion(f32[16,4,128]{2,1,0:T(4,128)} %fusion.97, f32[16,4,128]{2,1,0:T(4,128)} %get-tuple-element.11, f32[16,4]{1,0:T(8,128)} %copy.306, f32[16,4,128]{2,1,0:T(4,128)} %fusion.98, f32[16,4,128]{2,1,0:T(4,128)} %get-tuple-element.18, f32[16,4]{1,0:T(8,128)} %copy.304, pred[16]{0:T(512)(128)(4,1)} %get-tuple-element.64, ...), kind=kLoop, calls=%fused_computation.8 | loop fusion | flops 41943040 | bytes 8915072 | tf_op jit(solution)/shard_map/jit(_where)/select_n | solution.py:216
  457.6 15.8 %add_select_fusion = f32[16,4,128,128]{3,2,1,0:T(8,128)} fusion(f32[16,4,128]{2,1,0:T(4,128)} %fusion.97, f32[16,4,128]{2,1,0:T(4,128)} %get-tuple-element.11, f32[16,4]{1,0:T(8,128)} %copy.306, f32[16,4,128]{2,1,0:T(4,128)} %fusion.98, f32[16,4,128,128]{3,2,1,0:T(8,128)} %copy-done.5, f32[16,4,128]{2,1,0:T(4,128)} %get-tuple-element.18, f32[16,4]{1,0:T(8,128)} %copy.304, ...), kind=kLoop, calls=%fused_computation.6 | loop fusion | flops 47185920 | bytes 13109888 | tf_op jit(solution)/shard_map/jit(_where)/select_n | solution.py:217
  (308 shorter events, 108.1 us)
Async XLA Ops:
  7.2 426.4 %copy-start = (bf16[1408,1024]{1,0:T(8,128)(2,1)S(1)}, bf16[1408,1024]{1,0:T(8,128)(2,1)}, u32[]{:S(2)}) copy-start(bf16[1408,1024]{1,0:T(8,128)(2,1)} %param.43) | copy-start | bytes 8650756
  8.7 24.1 %all-to-all-start = ((s32[16,3,1]{1,2,0:T(1,128)}), s32[16,3,1]{1,2,0:T(1,128)S(1)}, u32[]{:S(2)}, u32[]{:S(2)}) async-start(s32[16,3,1]{1,2,0:T(1,128)} %bitcast.37), calls=%async_computation | async-start | bytes 16384 | tf_op jit(solution)/shard_map/all_to_all | solution.py:152
  33.3 301.3 %all-to-all-start.1 = ((bf16[48,2,128,512]{2,3,1,0:T(8,128)(2,1)}), bf16[48,2,128,512]{2,3,1,0:T(8,128)(2,1)}, u32[]{:S(2)}, u32[]{:S(2)}) async-start(bf16[48,2,128,512]{2,3,1,0:T(8,128)(2,1)} %copy.265), calls=%async_computation.1 | async-start | bytes 25165824 | tf_op jit(solution)/shard_map/all_to_all | solution.py:150
  39.4 365.3 %reduce-scatter.3.cloned.1.call-start = ((), (), s32[]{:S(2)}) async-start(), calls=%async_computation.4 | async-start | bytes 1572864 | tf_op jit(solution)/shard_map/reduce_scatter | solution.py:182
  40.4 100.0 %collective-permute-start = (s32[3]{0:T(128)}, s32[3]{0:T(128)}, u32[]{:S(2)}, u32[]{:S(2)}) collective-permute-start(s32[3]{0:T(128)} %get-tuple-element.57), channel_id=1, source_target_pairs={{0,2},{2,0},{4,6},{6,4},{8,10},{10,8},{12,14},{14,12},{16,18},{18,... | collective-permute-start | bytes 44 | tf_op jit(solution)/shard_map/ppermute | solution.py:35
  40.7 102.2 %collective-permute-start.1 = (s32[3]{0:T(128)}, s32[3]{0:T(128)}, u32[]{:S(2)}, u32[]{:S(2)}) collective-permute-start(s32[3]{0:T(128)} %get-tuple-element.56), channel_id=1, source_target_pairs={{0,4},{2,6},{4,0},{6,2},{8,12},{10,14},{12,8},{14,10},{16,20},{18,... | collective-permute-start | bytes 44 | tf_op jit(solution)/shard_map/ppermute | solution.py:35
  42.4 100.6 %collective-permute-start.2 = (s32[3]{0:T(128)}, s32[3]{0:T(128)}, u32[]{:S(2)}, u32[]{:S(2)}) collective-permute-start(s32[3]{0:T(128)} %get-tuple-element.55), channel_id=1, source_target_pairs={{0,6},{2,4},{4,2},{6,0},{8,14},{10,12},{12,10},{14,8},{16,22},{18,... | collective-permute-start | bytes 44 | tf_op jit(solution)/shard_map/ppermute | solution.py:35
  42.4 200.5 %collective-permute-start.3 = (s32[3]{0:T(128)}, s32[3]{0:T(128)}, u32[]{:S(2)}, u32[]{:S(2)}) collective-permute-start(s32[3]{0:T(128)} %get-tuple-element.54), channel_id=1, source_target_pairs={{0,8},{2,10},{4,12},{6,14},{8,0},{10,2},{12,4},{14,6},{16,24},{18,... | collective-permute-start | bytes 44 | tf_op jit(solution)/shard_map/ppermute | solution.py:35
  44.1 202.5 %collective-permute-start.4 = (s32[3]{0:T(128)}, s32[3]{0:T(128)}, u32[]{:S(2)}, u32[]{:S(2)}) collective-permute-start(s32[3]{0:T(128)} %get-tuple-element.53), channel_id=1, source_target_pairs={{0,10},{2,8},{4,14},{6,12},{8,2},{10,0},{12,6},{14,4},{16,26},{18,... | collective-permute-start | bytes 44 | tf_op jit(solution)/shard_map/ppermute | solution.py:35
  73.9 55.6 %copy-start.28 = (f32[16,4]{1,0:T(8,128)}, f32[16,4]{1,0:T(8,128)S(1)}, u32[]{:S(2)}) copy-start(f32[16,4]{1,0:T(8,128)S(1)} %copy.291) | copy-start | bytes 772
  88.1 47.1 %copy-start.60 = (pred[16]{0:T(512)(128)(4,1)}, pred[16]{0:T(512)(128)(4,1)S(1)}, u32[]{:S(2)}) copy-start(pred[16]{0:T(512)(128)(4,1)S(1)} %get-tuple-element.62) | copy-start | bytes 52
  135.3 107.6 %copy-start.76 = (s32[3]{0:T(128)S(1)}, s32[3]{0:T(128)}, u32[]{:S(2)}) copy-start(s32[3]{0:T(128)} %get-tuple-element.49) | copy-start | bytes 40
  135.3 111.3 %copy-start.75 = (s32[3]{0:T(128)S(1)}, s32[3]{0:T(128)}, u32[]{:S(2)}) copy-start(s32[3]{0:T(128)} %get-tuple-element.48) | copy-start | bytes 40
  135.4 113.1 %copy-start.74 = (s32[3]{0:T(128)S(1)}, s32[3]{0:T(128)}, u32[]{:S(2)}) copy-start(s32[3]{0:T(128)} %get-tuple-element.47) | copy-start | bytes 40
  135.4 115.4 %copy-start.73 = (s32[3]{0:T(128)S(1)}, s32[3]{0:T(128)}, u32[]{:S(2)}) copy-start(s32[3]{0:T(128)} %get-tuple-element.46) | copy-start | bytes 40
  135.4 177.9 %copy-start.72 = (s32[3]{0:T(128)S(1)}, s32[3]{0:T(128)}, u32[]{:S(2)}) copy-start(s32[3]{0:T(128)} %get-tuple-element.45) | copy-start | bytes 40
  135.4 178.2 %copy-start.71 = (s32[3]{0:T(128)S(1)}, s32[3]{0:T(128)}, u32[]{:S(2)}) copy-start(s32[3]{0:T(128)} %get-tuple-element.44) | copy-start | bytes 40
  135.4 181.6 %copy-start.70 = (s32[3]{0:T(128)S(1)}, s32[3]{0:T(128)}, u32[]{:S(2)}) copy-start(s32[3]{0:T(128)} %get-tuple-element.43) | copy-start | bytes 40
  140.3 108.2 %collective-permute-start.5 = (s32[3]{0:T(128)S(1)}, s32[3]{0:T(128)S(1)}, u32[]{:S(2)}, u32[]{:S(2)}) collective-permute-start(s32[3]{0:T(128)S(1)} %copy-done.79), channel_id=1, source_target_pairs={{0,12},{2,14},{4,8},{6,10},{8,4},{10,6},{12,0},{14,2},{16,28},{18,... | collective-permute-start | bytes 44 | tf_op jit(solution)/shard_map/ppermute | solution.py:35
  143.0 107.8 %collective-permute-start.6 = (s32[3]{0:T(128)S(1)}, s32[3]{0:T(128)S(1)}, u32[]{:S(2)}, u32[]{:S(2)}) collective-permute-start(s32[3]{0:T(128)S(1)} %copy-done.78), channel_id=1, source_target_pairs={{0,14},{2,12},{4,10},{6,8},{8,6},{10,4},{12,2},{14,0},{16,30},{18,... | collective-permute-start | bytes 44 | tf_op jit(solution)/shard_map/ppermute | solution.py:35
  143.0 170.2 %collective-permute-start.7 = (s32[3]{0:T(128)S(1)}, s32[3]{0:T(128)S(1)}, u32[]{:S(2)}, u32[]{:S(2)}) collective-permute-start(s32[3]{0:T(128)S(1)} %copy-done.77), channel_id=1, source_target_pairs={{0,16},{2,18},{4,20},{6,22},{8,24},{10,26},{12,28},{14,30},{16,0},... | collective-permute-start | bytes 44 | tf_op jit(solution)/shard_map/ppermute | solution.py:35
  242.9 70.7 %collective-permute-start.8 = (s32[3]{0:T(128)S(1)}, s32[3]{0:T(128)S(1)}, u32[]{:S(2)}, u32[]{:S(2)}) collective-permute-start(s32[3]{0:T(128)S(1)} %copy-done.76), channel_id=1, source_target_pairs={{0,18},{2,16},{4,22},{6,20},{8,26},{10,24},{12,30},{14,28},{16,2},... | collective-permute-start | bytes 44 | tf_op jit(solution)/shard_map/ppermute | solution.py:35
  246.6 70.3 %collective-permute-start.9 = (s32[3]{0:T(128)S(1)}, s32[3]{0:T(128)S(1)}, u32[]{:S(2)}, u32[]{:S(2)}) collective-permute-start(s32[3]{0:T(128)S(1)} %copy-done.75), channel_id=1, source_target_pairs={{0,20},{2,22},{4,16},{6,18},{8,28},{10,30},{12,24},{14,26},{16,4},... | collective-permute-start | bytes 44 | tf_op jit(solution)/shard_map/ppermute | solution.py:35
  248.5 74.2 %copy-start.80 = (s32[3]{0:T(128)}, s32[3]{0:T(128)S(1)}, u32[]{:S(2)}) copy-start(s32[3]{0:T(128)S(1)} %collective-permute-done.5) | copy-start | bytes 40
  248.5 70.5 %collective-permute-start.10 = (s32[3]{0:T(128)S(1)}, s32[3]{0:T(128)S(1)}, u32[]{:S(2)}, u32[]{:S(2)}) collective-permute-start(s32[3]{0:T(128)S(1)} %copy-done.74), channel_id=1, source_target_pairs={{0,22},{2,20},{4,18},{6,16},{8,30},{10,28},{12,26},{14,24},{16,6},... | collective-permute-start | bytes 44 | tf_op jit(solution)/shard_map/ppermute | solution.py:35
  250.7 72.0 %copy-start.81 = (s32[3]{0:T(128)}, s32[3]{0:T(128)S(1)}, u32[]{:S(2)}) copy-start(s32[3]{0:T(128)S(1)} %collective-permute-done.6) | copy-start | bytes 40
  250.7 68.2 %collective-permute-start.11 = (s32[3]{0:T(128)S(1)}, s32[3]{0:T(128)S(1)}, u32[]{:S(2)}, u32[]{:S(2)}) collective-permute-start(s32[3]{0:T(128)S(1)} %copy-done.73), channel_id=1, source_target_pairs={{0,24},{2,26},{4,28},{6,30},{8,16},{10,18},{12,20},{14,22},{16,8},... | collective-permute-start | bytes 44 | tf_op jit(solution)/shard_map/ppermute | solution.py:35
  313.2 5.7 %collective-permute-start.12 = (s32[3]{0:T(128)S(1)}, s32[3]{0:T(128)S(1)}, u32[]{:S(2)}, u32[]{:S(2)}) collective-permute-start(s32[3]{0:T(128)S(1)} %copy-done.72), channel_id=1, source_target_pairs={{0,26},{2,24},{4,30},{6,28},{8,18},{10,16},{12,22},{14,20},{16,10}... | collective-permute-start | bytes 44 | tf_op jit(solution)/shard_map/ppermute | solution.py:35
  313.6 6.3 %collective-permute-start.13 = (s32[3]{0:T(128)S(1)}, s32[3]{0:T(128)S(1)}, u32[]{:S(2)}, u32[]{:S(2)}) collective-permute-start(s32[3]{0:T(128)S(1)} %copy-done.71), channel_id=1, source_target_pairs={{0,28},{2,30},{4,24},{6,26},{8,20},{10,22},{12,16},{14,18},{16,12}... | collective-permute-start | bytes 44 | tf_op jit(solution)/shard_map/ppermute | solution.py:35
  317.0 5.7 %collective-permute-start.14 = (s32[3]{0:T(128)S(1)}, s32[3]{0:T(128)S(1)}, u32[]{:S(2)}, u32[]{:S(2)}) collective-permute-start(s32[3]{0:T(128)S(1)} %copy-done.70), channel_id=1, source_target_pairs={{0,30},{2,28},{4,26},{6,24},{8,22},{10,20},{12,18},{14,16},{16,14}... | collective-permute-start | bytes 44 | tf_op jit(solution)/shard_map/ppermute | solution.py:35
  384.1 43.9 %all-gather.2.cloned.1.call-start = ((), (), s32[]{:S(2)}) async-start(), calls=%async_computation.5 | async-start | bytes 1572864 | tf_op jit(solution)/shard_map/all_gather | solution.py:191
  407.9 65.4 %reduce-scatter.5.cloned.1.call-start = ((), (), s32[]{:S(2)}) async-start(), calls=%async_computation.6 | async-start | bytes 1572864 | tf_op jit(solution)/shard_map/reduce_scatter | solution.py:195
  (80 other events, 712.9 us)
Sparse Core Ops, SparseCore 0:
  384.2 18.9 reduce-scatter.2
  408.0 19.9 all-gather.1
  441.1 20.3 reduce-scatter.4
